TPU v7x, 512 devices: a whole 4x8x8 slice. The times are simulated.
512 devices in a mesh: dp: 16 (over y, core), tensor: 32 (over z, x).
Axes of the slice: x: 4, y: 8, z: 8, core: 2. Of those that a mesh axis runs over, the one named last changes fastest.
Arguments:
- tokens: bfloat16 [5632, 4096], P('dp', 'tensor'), may hold values from -6 to 6
- grad_out: bfloat16 [5632, 4096], P('dp', 'tensor'), may hold values from -6 to 6
- routes: float32 [16, 2, 16], P('dp'), may hold values from 0.005 to 0.3
- counts: int32 [16], P('dp'), may hold values from 176 to 352
- up_weight: bfloat16 [16, 4096, 4096], P(None, 'dp', 'tensor'), may hold values from -0.09375 to 0.09375
- down_weight: bfloat16 [16, 4096, 4096], P(None, 'tensor', 'dp'), may hold values from -0.09375 to 0.09375
Outputs:
- input_grad: bfloat16 [5632, 4096], P('dp', 'tensor')
- up_grad: bfloat16 [16, 4096, 4096], P(None, 'dp', 'tensor')
- down_grad: bfloat16 [16, 4096, 4096], P(None, 'tensor', 'dp')
- route_grad: float32 [16, 2, 16], P('dp')
Inputs may be any that keep to these rules, and one draw needn't show every extreme that they name: `counts`: the valid tokens of a data group, at least one whole segment.
All inputs are finite; a program needn't handle non-finite values.
Results may differ from a plain program's by a relative error of at most 0.02.
Values may be sent and summed in bfloat16 or wider, within the bound.
No kernel may reach another device: no remote copies, remote signals or barrier semaphores. Data moves between devices by JAX's collectives and lax.ppermute only.
A program may use at most 64 MiB of HBM per device.

v0:
```python
import jax
import jax.numpy as jnp
from jax import lax
from jax.sharding import PartitionSpec as P

gelu_scale = 0.7978845608
gelu_cubic = 0.044715


def gelu_pair(inputs):
    inner = gelu_scale * (inputs + gelu_cubic * inputs * inputs * inputs)
    tangent = jnp.tanh(inner)
    activated = 0.5 * inputs * (1.0 + tangent)
    derivative = 0.5 * (1.0 + tangent) + 0.5 * inputs * (1.0 - tangent * tangent) * gelu_scale * (
        1.0 + 3.0 * gelu_cubic * inputs * inputs
    )
    return (activated, derivative)


def body(tokens, grad_out, routes, counts, up_weight, down_weight):
    group_rows = tokens.shape[0]
    experts = up_weight.shape[0]
    segments = routes.shape[1]
    seg_rows = group_rows // segments
    high = lax.Precision.HIGHEST
    valid = (jnp.arange(group_rows, dtype=jnp.int32) < counts[0])[:, None]
    masked = jnp.where(valid, grad_out, jnp.zeros_like(grad_out))
    full_tokens, full_grads = (
        lax.all_gather(tokens, "tensor", axis=1, tiled=True),
        lax.all_gather(masked, "tensor", axis=1, tiled=True),
    )
    all_routes = lax.all_gather(routes, "dp", axis=0, tiled=True)
    flat_routes = all_routes.reshape(-1, experts)
    local_up = jnp.dot(
        flat_routes, up_weight.reshape(experts, -1).astype(jnp.float32), precision=high
    )
    local_up = local_up.reshape((-1,) + up_weight.shape[1:]).astype(jnp.bfloat16)
    down_turned = jnp.swapaxes(down_weight, 1, 2)
    local_down = jnp.dot(
        flat_routes, down_turned.reshape(experts, -1).astype(jnp.float32), precision=high
    )
    local_down = local_down.reshape((-1,) + down_turned.shape[1:]).astype(jnp.bfloat16)
    merged_up, merged_down = (
        lax.all_to_all(local_up, "dp", split_axis=0, concat_axis=1, tiled=True),
        lax.all_to_all(local_down, "dp", split_axis=0, concat_axis=1, tiled=True),
    )
    down_terms = []
    slopes = []
    for segment in range(segments):
        seg_tokens = full_tokens[segment * seg_rows : (segment + 1) * seg_rows]
        seg_grads = full_grads[segment * seg_rows : (segment + 1) * seg_rows]
        pre = jnp.dot(seg_tokens, merged_up[segment], preferred_element_type=jnp.float32)
        activated, derivative = gelu_pair(pre)
        activated = activated.astype(jnp.bfloat16)
        slopes.append(derivative)
        down_terms.append(
            jnp.einsum(
                "rd,rh->dh", seg_grads, activated, preferred_element_type=jnp.float32
            ).astype(jnp.bfloat16)
        )
    down_stack = jnp.stack(down_terms, axis=0)
    up_terms = []
    hidden_grads = []
    for segment in range(segments):
        seg_tokens = full_tokens[segment * seg_rows : (segment + 1) * seg_rows]
        seg_grads = full_grads[segment * seg_rows : (segment + 1) * seg_rows]
        back = jnp.einsum(
            "rd,dh->rh", seg_grads, merged_down[segment], preferred_element_type=jnp.float32
        )
        hidden_grad = (back * slopes[segment]).astype(jnp.bfloat16)
        hidden_grads.append(hidden_grad)
        up_terms.append(
            jnp.einsum(
                "rd,rh->dh", seg_tokens, hidden_grad, preferred_element_type=jnp.float32
            ).astype(jnp.bfloat16)
        )
    up_stack = jnp.stack(up_terms, axis=0)
    recv_up, recv_down = (
        lax.all_to_all(up_stack, "dp", split_axis=1, concat_axis=0, tiled=True),
        lax.all_to_all(down_stack, "dp", split_axis=1, concat_axis=0, tiled=True),
    )
    partials = [
        jnp.einsum(
            "rh,dh->rd",
            hidden_grads[segment],
            merged_up[segment],
            preferred_element_type=jnp.float32,
        )
        for segment in range(segments)
    ]
    rounded = lax.optimization_barrier(jnp.concatenate(partials, axis=0).astype(jnp.bfloat16))
    summed = lax.psum_scatter(
        rounded.astype(jnp.float32).astype(jnp.bfloat16), "tensor", scatter_dimension=1, tiled=True
    )
    up_grad = jnp.einsum(
        "ke,kdh->edh", flat_routes, recv_up.astype(jnp.float32), precision=high
    ).astype(jnp.bfloat16)
    down_grad = jnp.einsum(
        "ke,kdh->ehd", flat_routes, recv_down.astype(jnp.float32), precision=high
    ).astype(jnp.bfloat16)
    inner_sums = jnp.einsum("kdh,edh->ke", recv_up, up_weight, preferred_element_type=jnp.float32)
    inner_sums = inner_sums + jnp.einsum(
        "kdh,ehd->ke", recv_down, down_weight, preferred_element_type=jnp.float32
    )
    table = inner_sums.reshape(all_routes.shape)
    totals = lax.psum(table, ("dp", "tensor"))
    route_grad = lax.dynamic_slice_in_dim(totals, lax.axis_index("dp"), 1, 0)
    return (summed, up_grad, down_grad, route_grad)


def solution(mesh):
    return jax.shard_map(
        body,
        mesh=mesh,
        in_specs=(
            P("dp", "tensor"),
            P("dp", "tensor"),
            P("dp", None, None),
            P("dp"),
            P(None, "dp", "tensor"),
            P(None, "tensor", "dp"),
        ),
        out_specs=(
            P("dp", "tensor"),
            P(None, "dp", "tensor"),
            P(None, "tensor", "dp"),
            P("dp", None, None),
        ),
        check_vma=False,
    )
```

profile of v0, /device:TPU:8, one launch (start us, length us, event | category | flops | bytes accessed | tf_op | source)
XLA Modules:
  0.0 445.9 jit_solution(14864564712320135347)
XLA Ops:
  7.9 20.2 %all_gather.10 = f32[16,2,16]{2,1,0:T(2,128)S(1)} all-gather(f32[1,2,16]{2,1,0:T(2,128)} %param.8), channel_id=1, replica_groups=mesh['dp'=16,'tensor'=32] {'dp'}, dimensions={0}, use_global_device_ids=true | all-gather | bytes 2176 | tf_op jit(solution)/shard_map/all_gather | solution.py:32
  28.1 3.1 convolution_convert_fusion.6
  31.2 2.2 copy.65
  33.4 3.8 all-to-all-start.1
  42.1 2.2 copy.62
  44.3 40.2 %all-to-all-done.1 = bf16[32,256,128]{2,1,0:T(8,128)(2,1)S(1)} async-done(((bf16[32,256,128]{2,1,0:T(8,128)(2,1)}), bf16[32,256,128]{2,1,0:T(8,128)(2,1)S(1)}, u32[]{:S(2)}, u32[]{:S(2)}) %all-to-all-start.1) | async-done | bytes 2097184 | tf_op jit(solution)/shard_map/all_to_all | solution.py:44
  84.5 6.6 %all-to-all-start = ((bf16[32,256,128]{2,1,0:T(8,128)(2,1)}), bf16[32,256,128]{2,1,0:T(8,128)(2,1)}, u32[]{:S(2)}, u32[]{:S(2)}) async-start(bf16[32,256,128]{2,1,0:T(8,128)(2,1)} %copy.62), calls=%async_computation | async-start | bytes 4194304 | tf_op jit(solution)/shard_map/all_to_all | solution.py:45
  92.3 46.3 %all-to-all-done = bf16[32,256,128]{2,1,0:T(8,128)(2,1)} async-done(((bf16[32,256,128]{2,1,0:T(8,128)(2,1)}), bf16[32,256,128]{2,1,0:T(8,128)(2,1)}, u32[]{:S(2)}, u32[]{:S(2)}) %all-to-all-start) | async-done | bytes 2097184 | tf_op jit(solution)/shard_map/all_to_all | solution.py:45
  138.6 2.8 fusion.99
  143.3 43.1 %all-gather.3.cloned.1.call-done = bf16[352,4096]{1,0:T(8,128)(2,1)} async-done(((bf16[352,128]{1,0:T(8,128)(2,1)}), bf16[352,4096]{1,0:T(8,128)(2,1)}) %all-gather.3.cloned.1.call-update) | async-done | bytes 2883600 | tf_op jit(solution)/shard_map/all_gather | solution.py:30
  186.4 2.3 fusion.51
  192.0 3.8 copy.66
  195.8 7.3 %all-to-all-start.2 = ((bf16[2,4096,128]{2,0,1:T(2,128)(2,1)}), bf16[2,4096,128]{2,0,1:T(2,128)(2,1)S(1)}, u32[]{:S(2)}, u32[]{:S(2)}) async-start(bf16[2,4096,128]{2,0,1:T(2,128)(2,1)} %copy.66), calls=%async_computation.2 | async-start | bytes 4194304 | tf_op jit(solution)/shard_map/all_to_all | solution.py:79
  207.4 4.6 %copy.95 = bf16[352,4096]{0,1:T(8,128)(2,1)} copy(bf16[352,4096]{1,0:T(8,128)(2,1)} %pad_maximum_fusion) | data formatting | bytes 5767168
  212.0 2.1 fusion.2
  214.2 2.1 fusion.3
  216.5 18.1 %copy.70 = bf16[2,4096,128]{2,0,1:T(2,128)(2,1)} copy(bf16[2,4096,128]{2,1,0:T(8,128)(2,1)S(1)} %pad_maximum_fusion.2) | data formatting | bytes 4194304 | tf_op jit(solution)/shard_map/stack | solution.py:61
  234.6 15.8 %all-to-all-done.2 = bf16[2,4096,128]{2,0,1:T(2,128)(2,1)S(1)} async-done(((bf16[2,4096,128]{2,0,1:T(2,128)(2,1)}), bf16[2,4096,128]{2,0,1:T(2,128)(2,1)S(1)}, u32[]{:S(2)}, u32[]{:S(2)}) %all-to-all-start.2) | async-done | bytes 2097184 | tf_op jit(solution)/shard_map/all_to_all | solution.py:79
  250.4 6.5 %all-to-all-start.3 = ((bf16[2,4096,128]{2,0,1:T(2,128)(2,1)}), bf16[2,4096,128]{2,0,1:T(2,128)(2,1)}, u32[]{:S(2)}, u32[]{:S(2)}) async-start(bf16[2,4096,128]{2,0,1:T(2,128)(2,1)} %copy.70), calls=%async_computation.3 | async-start | bytes 4194304 | tf_op jit(solution)/shard_map/all_to_all | solution.py:80
  260.7 43.8 %all-to-all-done.3 = bf16[2,4096,128]{2,0,1:T(2,128)(2,1)} async-done(((bf16[2,4096,128]{2,0,1:T(2,128)(2,1)}), bf16[2,4096,128]{2,0,1:T(2,128)(2,1)}, u32[]{:S(2)}, u32[]{:S(2)}) %all-to-all-start.3) | async-done | bytes 2097184 | tf_op jit(solution)/shard_map/all_to_all | solution.py:80
  304.5 2.3 copy.94
  313.6 3.5 fusion.21
  318.6 98.9 %psum.7 = f32[16,2,16]{2,1,0:T(2,128)S(1)} all-reduce(f32[16,2,16]{2,1,0:T(2,128)S(1)} %bitcast.141), channel_id=1, replica_groups=mesh['dp'=16,'tensor'=32] {'dp','tensor'}, use_global_device_ids=true, to_apply=%region_1.2 | all-reduce | flops 512 | bytes 4096 | tf_op jit(solution)/shard_map/psum | solution.py:106
  418.1 19.6 %reduce-scatter.4.cloned.1.call-done = bf16[128,352]{1,0:T(8,128)(2,1)} async-done(((bf16[4096,352]{1,0:T(8,128)(2,1)}), bf16[128,352]{1,0:T(8,128)(2,1)}) %reduce-scatter.4.cloned.1.call-update) | async-done | bytes 90128
  (48 shorter events, 30.1 us)
Async XLA Ops:
  7.2 134.2 %all-gather.5.cloned.1.call-start = ((), (), s32[]{:S(2)}) async-start(), calls=%async_computation.6 | async-start | bytes 2973696 | tf_op jit(solution)/shard_map/all_gather | solution.py:29
  33.4 4.5 %copy-start.7 = (bf16[352,128]{1,0:T(8,128)(2,1)S(1)}, bf16[352,128]{1,0:T(8,128)(2,1)}, u32[]{:S(2)}) copy-start(bf16[352,128]{1,0:T(8,128)(2,1)} %param.7) | copy-start | bytes 270340
  33.4 51.2 %all-to-all-start.1 = ((bf16[32,256,128]{2,1,0:T(8,128)(2,1)}), bf16[32,256,128]{2,1,0:T(8,128)(2,1)S(1)}, u32[]{:S(2)}, u32[]{:S(2)}) async-start(bf16[32,256,128]{2,1,0:T(8,128)(2,1)} %copy.65), calls=%async_computation.1 | async-start | bytes 4194304 | tf_op jit(solution)/shard_map/all_to_all | solution.py:44
  37.1 149.3 %all-gather.3.cloned.1.call-start = ((), (), s32[]{:S(2)}) async-start(), calls=%async_computation.5 | async-start | bytes 2973696 | tf_op jit(solution)/shard_map/all_gather | solution.py:30
  84.5 54.1 %all-to-all-start = ((bf16[32,256,128]{2,1,0:T(8,128)(2,1)}), bf16[32,256,128]{2,1,0:T(8,128)(2,1)}, u32[]{:S(2)}, u32[]{:S(2)}) async-start(bf16[32,256,128]{2,1,0:T(8,128)(2,1)} %copy.62), calls=%async_computation | async-start | bytes 4194304 | tf_op jit(solution)/shard_map/all_to_all | solution.py:45
  138.6 2.8 copy-start.1
  186.4 2.6 copy-start.3
  189.0 1.8 copy-start.2
  195.8 54.7 %all-to-all-start.2 = ((bf16[2,4096,128]{2,0,1:T(2,128)(2,1)}), bf16[2,4096,128]{2,0,1:T(2,128)(2,1)S(1)}, u32[]{:S(2)}, u32[]{:S(2)}) async-start(bf16[2,4096,128]{2,0,1:T(2,128)(2,1)} %copy.66), calls=%async_computation.2 | async-start | bytes 4194304 | tf_op jit(solution)/shard_map/all_to_all | solution.py:79
  203.1 234.7 %reduce-scatter.4.cloned.1.call-start = ((), (), s32[]{:S(2)}) async-start(), calls=%async_computation.7 | async-start | bytes 3244032
  234.6 22.4 %copy-start = (bf16[16,128,256]{2,1,0:T(8,128)(2,1)S(1)}, bf16[16,128,256]{2,1,0:T(8,128)(2,1)}, u32[]{:S(2)}) copy-start(bf16[16,128,256]{2,1,0:T(8,128)(2,1)} %param.11) | copy-start | bytes 3145732
  250.4 54.0 %all-to-all-start.3 = ((bf16[2,4096,128]{2,0,1:T(2,128)(2,1)}), bf16[2,4096,128]{2,0,1:T(2,128)(2,1)}, u32[]{:S(2)}, u32[]{:S(2)}) async-start(bf16[2,4096,128]{2,0,1:T(2,128)(2,1)} %copy.70), calls=%async_computation.3 | async-start | bytes 4194304 | tf_op jit(solution)/shard_map/all_to_all | solution.py:80
  304.5 2.3 copy-start.4
  304.5 2.5 copy-start.5
  306.7 2.3 copy-start.6
Sparse Core Ops, SparseCore 0:
  11.0 88.2 all-gather.4
  103.0 83.3 all-gather.2
  212.1 225.5 reduce-scatter.3
where the time goes:
time: 447 us; the launch traced here: 446 us
  waiting for transfers between devices  210 us (47%)
  blocking collectives  119 us (27%)
  local copies, waits for them, and re-layouts  48.7 us (11%)
  matrix products  26.5 us (6%)
  starting transfers between devices  24.5 us (5%)
  between operations  14.6 us (3%)
    psum x1, blocking collectives, body(): totals = lax.psum(table, ('dp', 'tensor'))  98.9 us
    all_to_all x1, waiting for transfers between devices, body(): lax.all_to_all(local_down, 'dp', split_axis=0, concat_axis=1, tiled=True)  46.3 us
    all_to_all x1, waiting for transfers between devices, body(): lax.all_to_all(down_stack, 'dp', split_axis=1, concat_axis=0, tiled=True)  43.8 us
    all_gather x1, waiting for transfers between devices, body(): lax.all_gather(masked, 'tensor', axis=1, tiled=True)  43.1 us
    all_to_all x1, waiting for transfers between devices, body(): lax.all_to_all(local_up, 'dp', split_axis=0, concat_axis=1, tiled=True)  40.2 us
    unnamed x4, waiting for transfers between devices  20.4 us
    all_gather x1, blocking collectives, body(): all_routes = lax.all_gather(routes, 'dp', axis=0, tiled=True)  20.2 us
    another operation x1, local copies, waits for them, and re-layouts, body(): down_stack = jnp.stack(down_terms, axis=0)  18.1 us
  transfers between devices with their start and end apart: 7, of which 6 were waited for; matrix products, arithmetic and copies ran while one was open for 15% of the time, Pallas kernels for 0%

commit v1 on v0

--- a/solution.py
+++ b/solution.py
@@ -29,7 +29,12 @@
         lax.all_gather(tokens, "tensor", axis=1, tiled=True),
         lax.all_gather(masked, "tensor", axis=1, tiled=True),
     )
-    all_routes = lax.all_gather(routes, "dp", axis=0, tiled=True)
+    ring = [routes]
+    for hop in range(15):
+        ring.append(lax.ppermute(ring[-1], "dp", [(dev, (dev + 1) % 16) for dev in range(16)]))
+    all_routes = jnp.roll(
+        jnp.concatenate(ring[::-1], axis=0), (lax.axis_index("dp") + 1) * ring[0].shape[0], axis=0
+    )
     flat_routes = all_routes.reshape(-1, experts)
     local_up = jnp.dot(
         flat_routes, up_weight.reshape(experts, -1).astype(jnp.float32), precision=high

time: 447 us -> 455 us (1.018)
  waiting for transfers between devices: 210 us -> 230 us
  blocking collectives: 119 us -> 102 us
  starting transfers between devices: 24.5 us -> 30.2 us
    ppermute x0 -> x15, waiting for transfers between devices: none -> 63.2 us  [body(): lax.ppermute(ring[-1], 'dp', [(dev, (dev + 1) % 16) for dev in range(16)])]
    all_gather x1, waiting for transfers between devices: 43.1 us -> 0.02 us  [body(): lax.all_gather(masked, 'tensor', axis=1, tiled=True)]
    all_gather x1 -> x0, blocking collectives: 20.2 us -> none  [body(): all_routes = lax.all_gather(routes, 'dp', axis=0, tiled=True)]
    all_to_all x1, waiting for transfers between devices: 40.2 us -> 46 us  [body(): lax.all_to_all(local_up, 'dp', split_axis=0, concat_axis=1, tiled=True)]
    unnamed x21 -> x28, local copies, waits for them, and re-layouts: 12.1 us -> 13.1 us
  transfers between devices with their start and end apart: 7 -> 22, of which waited for: 6 -> 20; matrix products, arithmetic and copies ran while one was open for 15% -> 15% of each run, Pallas kernels for 0% -> 0%
where the time goes in v1:
time: 455 us
  waiting for transfers between devices  230 us (51%)
  blocking collectives  102 us (22%)
  local copies, waits for them, and re-layouts  49.3 us (11%)
  starting transfers between devices  30.2 us (7%)
  matrix products  25.4 us (6%)
  between operations  14.7 us (3%)
    psum x1, blocking collectives, body(): totals = lax.psum(table, ('dp', 'tensor'))  102 us
    ppermute x15, waiting for transfers between devices, body(): lax.ppermute(ring[-1], 'dp', [(dev, (dev + 1) % 16) for dev in range(16)])  63.2 us
    all_to_all x1, waiting for transfers between devices, body(): lax.all_to_all(local_up, 'dp', split_axis=0, concat_axis=1, tiled=True)  46 us
    all_to_all x1, waiting for transfers between devices, body(): lax.all_to_all(down_stack, 'dp', split_axis=1, concat_axis=0, tiled=True)  43.8 us
    all_to_all x1, waiting for transfers between devices, body(): lax.all_to_all(local_down, 'dp', split_axis=0, concat_axis=1, tiled=True)  41.8 us
    unnamed x4, waiting for transfers between devices  19 us
    another operation x1, local copies, waits for them, and re-layouts, body(): down_stack = jnp.stack(down_terms, axis=0)  18.1 us
    all_to_all x1, waiting for transfers between devices, body(): lax.all_to_all(up_stack, 'dp', split_axis=1, concat_axis=0, tiled=True)  15.8 us
  transfers between devices with their start and end apart: 22, of which 20 were waited for; matrix products, arithmetic and copies ran while one was open for 15% of the time, Pallas kernels for 0%

profile of v1, /device:TPU:8, one launch (start us, length us, event | category | flops | bytes accessed | tf_op | source)
XLA Modules:
  0.0 454.6 jit_solution(17942672451349439686)
XLA Ops:
  11.8 4.9 %collective-permute-done.1 = f32[1,2,16]{0,2,1:T(8,128)S(1)} collective-permute-done((f32[1,2,16]{0,2,1:T(8,128)S(1)}, f32[1,2,16]{0,2,1:T(8,128)S(1)}, u32[]{:S(2)}, u32[]{:S(2)}) %collective-permute-start.1) | collective-permute-done | bytes 160 | tf_op jit(solution)/shard_map/ppermute | solution.py:34
  16.7 4.4 collective-permute-done.2
  21.1 4.4 collective-permute-done.3
  25.5 4.4 collective-permute-done.4
  29.8 4.4 collective-permute-done.5
  38.6 4.4 collective-permute-done.7
  43.0 4.4 collective-permute-done.8
  47.3 4.4 collective-permute-done.9
  51.7 4.4 collective-permute-done.10
  56.1 4.4 collective-permute-done.11
  60.5 4.4 collective-permute-done.12
  64.8 4.4 collective-permute-done.13
  78.0 10.2 %all-to-all-start = ((bf16[32,256,128]{2,1,0:T(8,128)(2,1)}), bf16[32,256,128]{2,1,0:T(8,128)(2,1)S(1)}, u32[]{:S(2)}, u32[]{:S(2)}) async-start(bf16[32,256,128]{2,1,0:T(8,128)(2,1)} %copy.72), calls=%async_computation | async-start | bytes 4194304 | tf_op jit(solution)/shard_map/all_to_all | solution.py:50
  93.8 41.8 %all-to-all-done = bf16[32,256,128]{2,1,0:T(8,128)(2,1)S(1)} async-done(((bf16[32,256,128]{2,1,0:T(8,128)(2,1)}), bf16[32,256,128]{2,1,0:T(8,128)(2,1)S(1)}, u32[]{:S(2)}, u32[]{:S(2)}) %all-to-all-start) | async-done | bytes 2097184 | tf_op jit(solution)/shard_map/all_to_all | solution.py:50
  135.6 6.6 %all-to-all-start.1 = ((bf16[32,256,128]{2,1,0:T(8,128)(2,1)}), bf16[32,256,128]{2,1,0:T(8,128)(2,1)}, u32[]{:S(2)}, u32[]{:S(2)}) async-start(bf16[32,256,128]{2,1,0:T(8,128)(2,1)} %copy.75), calls=%async_computation.1 | async-start | bytes 4194304 | tf_op jit(solution)/shard_map/all_to_all | solution.py:49
  143.6 46.0 %all-to-all-done.1 = bf16[32,256,128]{2,1,0:T(8,128)(2,1)} async-done(((bf16[32,256,128]{2,1,0:T(8,128)(2,1)}), bf16[32,256,128]{2,1,0:T(8,128)(2,1)}, u32[]{:S(2)}, u32[]{:S(2)}) %all-to-all-start.1) | async-done | bytes 2097184 | tf_op jit(solution)/shard_map/all_to_all | solution.py:49
  203.0 6.6 %all-to-all-start.2 = ((bf16[2,4096,128]{2,0,1:T(2,128)(2,1)}), bf16[2,4096,128]{2,0,1:T(2,128)(2,1)S(1)}, u32[]{:S(2)}, u32[]{:S(2)}) async-start(bf16[2,4096,128]{2,0,1:T(2,128)(2,1)} %copy.76), calls=%async_computation.2 | async-start | bytes 4194304 | tf_op jit(solution)/shard_map/all_to_all | solution.py:84
  213.9 4.6 %copy.103 = bf16[352,4096]{0,1:T(8,128)(2,1)} copy(bf16[352,4096]{1,0:T(8,128)(2,1)} %pad_maximum_fusion) | data formatting | bytes 5767168
  223.0 18.1 %copy.79 = bf16[2,4096,128]{2,0,1:T(2,128)(2,1)} copy(bf16[2,4096,128]{2,1,0:T(8,128)(2,1)S(1)} %pad_maximum_fusion.2) | data formatting | bytes 4194304 | tf_op jit(solution)/shard_map/stack | solution.py:66
  241.1 15.8 %all-to-all-done.2 = bf16[2,4096,128]{2,0,1:T(2,128)(2,1)S(1)} async-done(((bf16[2,4096,128]{2,0,1:T(2,128)(2,1)}), bf16[2,4096,128]{2,0,1:T(2,128)(2,1)S(1)}, u32[]{:S(2)}, u32[]{:S(2)}) %all-to-all-start.2) | async-done | bytes 2097184 | tf_op jit(solution)/shard_map/all_to_all | solution.py:84
  257.0 6.5 %all-to-all-start.3 = ((bf16[2,4096,128]{2,0,1:T(2,128)(2,1)}), bf16[2,4096,128]{2,0,1:T(2,128)(2,1)}, u32[]{:S(2)}, u32[]{:S(2)}) async-start(bf16[2,4096,128]{2,0,1:T(2,128)(2,1)} %copy.79), calls=%async_computation.3 | async-start | bytes 4194304 | tf_op jit(solution)/shard_map/all_to_all | solution.py:85
  267.2 43.8 %all-to-all-done.3 = bf16[2,4096,128]{2,0,1:T(2,128)(2,1)} async-done(((bf16[2,4096,128]{2,0,1:T(2,128)(2,1)}), bf16[2,4096,128]{2,0,1:T(2,128)(2,1)}, u32[]{:S(2)}, u32[]{:S(2)}) %all-to-all-start.3) | async-done | bytes 2097184 | tf_op jit(solution)/shard_map/all_to_all | solution.py:85
  325.2 102.4 %psum.7 = f32[16,2,16]{2,1,0:T(2,128)S(1)} all-reduce(f32[16,2,16]{2,1,0:T(2,128)S(1)} %bitcast.134), channel_id=1, replica_groups=mesh['dp'=16,'tensor'=32] {'dp','tensor'}, use_global_device_ids=true, to_apply=%region_1.2 | all-reduce | flops 512 | bytes 4096 | tf_op jit(solution)/shard_map/psum | solution.py:111
  428.2 18.2 %reduce-scatter.4.cloned.1.call-done = bf16[128,352]{1,0:T(8,128)(2,1)} async-done(((bf16[4096,352]{1,0:T(8,128)(2,1)}), bf16[128,352]{1,0:T(8,128)(2,1)}) %reduce-scatter.4.cloned.1.call-update) | async-done | bytes 90128
  (87 shorter events, 66.3 us)
Async XLA Ops:
  7.2 184.2 %all-gather.5.cloned.1.call-start = ((), (), s32[]{:S(2)}) async-start(), calls=%async_computation.6 | async-start | bytes 2973696 | tf_op jit(solution)/shard_map/all_gather | solution.py:29
  8.7 3.2 collective-permute-start
  11.8 4.9 %collective-permute-start.1 = (f32[1,2,16]{0,2,1:T(8,128)S(1)}, f32[1,2,16]{0,2,1:T(8,128)S(1)}, u32[]{:S(2)}, u32[]{:S(2)}) collective-permute-start(f32[1,2,16]{0,2,1:T(8,128)S(1)} %collective-permute-done), channel_id=1, source_target_pairs={{0,32},{32,64},{64,96},{96,128},{128,160},{160,192},{192,224},{224... | collective-permute-start | bytes 392 | tf_op jit(solution)/shard_map/ppermute | solution.py:34
  16.7 4.4 collective-permute-start.2
  21.1 4.4 collective-permute-start.3
  25.4 4.4 collective-permute-start.4
  29.8 4.4 collective-permute-start.5
  34.2 4.4 collective-permute-start.6
  38.6 4.4 collective-permute-start.7
  43.0 4.4 collective-permute-start.8
  47.3 4.4 collective-permute-start.9
  51.7 4.4 collective-permute-start.10
  56.1 4.4 collective-permute-start.11
  60.5 4.4 collective-permute-start.12
  64.8 4.4 collective-permute-start.13
  69.2 4.4 collective-permute-start.14
  78.0 11.7 %copy-start.5 = (bf16[16,256,128]{2,1,0:T(8,128)(2,1)S(1)}, bf16[16,256,128]{2,1,0:T(8,128)(2,1)}, u32[]{:S(2)}) copy-start(bf16[16,256,128]{2,1,0:T(8,128)(2,1)} %param.10) | copy-start | bytes 3145732
  78.0 57.6 %all-to-all-start = ((bf16[32,256,128]{2,1,0:T(8,128)(2,1)}), bf16[32,256,128]{2,1,0:T(8,128)(2,1)S(1)}, u32[]{:S(2)}, u32[]{:S(2)}) async-start(bf16[32,256,128]{2,1,0:T(8,128)(2,1)} %copy.72), calls=%async_computation | async-start | bytes 4194304 | tf_op jit(solution)/shard_map/all_to_all | solution.py:50
  88.2 105.5 %all-gather.3.cloned.1.call-start = ((), (), s32[]{:S(2)}) async-start(), calls=%async_computation.5 | async-start | bytes 2973696 | tf_op jit(solution)/shard_map/all_gather | solution.py:30
  135.6 54.1 %all-to-all-start.1 = ((bf16[32,256,128]{2,1,0:T(8,128)(2,1)}), bf16[32,256,128]{2,1,0:T(8,128)(2,1)}, u32[]{:S(2)}, u32[]{:S(2)}) async-start(bf16[32,256,128]{2,1,0:T(8,128)(2,1)} %copy.75), calls=%async_computation.1 | async-start | bytes 4194304 | tf_op jit(solution)/shard_map/all_to_all | solution.py:49
  203.0 53.9 %all-to-all-start.2 = ((bf16[2,4096,128]{2,0,1:T(2,128)(2,1)}), bf16[2,4096,128]{2,0,1:T(2,128)(2,1)S(1)}, u32[]{:S(2)}, u32[]{:S(2)}) async-start(bf16[2,4096,128]{2,0,1:T(2,128)(2,1)} %copy.76), calls=%async_computation.2 | async-start | bytes 4194304 | tf_op jit(solution)/shard_map/all_to_all | solution.py:84
  209.6 236.8 %reduce-scatter.4.cloned.1.call-start = ((), (), s32[]{:S(2)}) async-start(), calls=%async_computation.7 | async-start | bytes 3244032
  241.1 22.4 %copy-start = (bf16[16,128,256]{2,1,0:T(8,128)(2,1)S(1)}, bf16[16,128,256]{2,1,0:T(8,128)(2,1)}, u32[]{:S(2)}) copy-start(bf16[16,128,256]{2,1,0:T(8,128)(2,1)} %param.11) | copy-start | bytes 3145732
  257.0 54.0 %all-to-all-start.3 = ((bf16[2,4096,128]{2,0,1:T(2,128)(2,1)}), bf16[2,4096,128]{2,0,1:T(2,128)(2,1)}, u32[]{:S(2)}, u32[]{:S(2)}) async-start(bf16[2,4096,128]{2,0,1:T(2,128)(2,1)} %copy.79), calls=%async_computation.3 | async-start | bytes 4194304 | tf_op jit(solution)/shard_map/all_to_all | solution.py:85
  (9 other events, 31.0 us)
Sparse Core Ops, SparseCore 0:
  11.0 88.2 all-gather.4
  102.9 83.5 all-gather.2
  218.7 227.7 reduce-scatter.3
